TPU v7x, 256 devices: a whole 4x4x8 slice. The times are simulated.
256 devices in a mesh: tr: 32 (over y, z), los: 8 (over x, core).
Axes of the slice: x: 4, y: 4, z: 8, core: 2. Of those that a mesh axis runs over, the one named last changes fastest.
Arguments:
- flux: float32 [64, 65536], P('los', 'tr'), may hold values from -15 to 15
- noise_weight: float32 [64, 65536], P('los', 'tr'), may hold values from 0.2 to 5
- pixel_owner: int32 [65536, 1], P('tr'), may hold values from 0 to 31; in each aligned block of 2048 rows (0 to 2047, 2048 to 4095, ...) at most 128 rows name the same one
- pixel_cell: int32 [65536], P('tr'), may hold values from 0 to 8191
- plane_bin: int32 [64], replicated, may hold values from 0 to 7
- bin_coeffs: float32 [3, 8], replicated, may hold values from 0.25 to 4
Outputs:
- solution: float32 [64, 128, 2048], P('los', 'tr')
- residual: float32 [64, 128, 2048], P('los', 'tr')
Inputs may be any that keep to these rules, and one draw needn't show every extreme that they name: `pixel_owner`: among the 2048 pixel rows of one device along tr (aligned blocks) at most 128 name the same strip, a bound that some block reaches of them.
All inputs are finite; a program needn't handle non-finite values.
Results may differ from a plain program's by a relative error of at most 0.00045.
Values sent between devices are 32-bit elements; how exact they have to be, the bound alone decides.
A program may use at most 128 MiB of HBM per device.

v0:
```python
import functools

import jax
import jax.numpy as jnp
from jax import lax
from jax.experimental import pallas as pl
from jax.experimental.pallas import tpu as pltpu
from jax.sharding import PartitionSpec as P

MESH = pl.DeviceIdType.MESH
F32 = jnp.float32
BF16 = jnp.bfloat16
I32 = jnp.int32
SX = 4
CHUNK = 256
CAP = 128
MASS = 0.5
NT = (((1,), (1,)), ((), ()))


def iota(shape, dim):
    return lax.broadcasted_iota(I32, shape, dim)


def two_pieces(values):
    high = values.astype(BF16)
    return high, (values - high.astype(F32)).astype(BF16)


def roll(x, shift, axis):
    size = x.shape[axis]
    return pltpu.roll(x, shift % size if isinstance(shift, int) else shift, axis)


def kernel(
    n_tr, n_los, nzr, flux_ref, weight_ref, owner_ref, cell_ref, bin_ref, coef_ref,
    sol_ref, res_ref,
    xa, xb, pk, rv, acc, sb, tb, kxs, kys, lks, base, inv, gf, zf, qf, wf, sf,
    hs, hr, cs, cr, rb, ps, p1, p2,
    route_send, route_recv, in_send, in_recv, halo_send, halo_recv,
    out_send, out_recv, sum_send, sum_recv, fin_send, fin_recv,
):
    planes, pix = flux_ref.shape
    depth = planes * n_los
    half = depth // 2
    groups = depth // 4
    tr = lax.axis_index("tr")
    los = lax.axis_index("los")
    nyr = n_tr // nzr
    y, zc = tr // nzr, tr % nzr
    offsets = [(dy, dz) for dy in range(nyr) for dz in range(nzr)]
    offsets.sort(key=lambda o: (min(o[0], nyr - o[0]) + min(o[1], nzr - o[1]), o))

    def tr_peer(slot):
        dy, dz = offsets[slot]
        return ((y + dy) % nyr) * nzr + (zc + dz) % nzr

    def los_peer(step):
        return (los + step) % n_los

    def send(src, dst, ssem, rsem, at_tr, at_los):
        return pltpu.make_async_remote_copy(
            src_ref=src, dst_ref=dst, send_sem=ssem, recv_sem=rsem,
            device_id=(at_tr, at_los), device_id_type=MESH,
        )

    @pl.when(tr == 0)
    def _():
        for turn in range(2):
            hr[turn, 0] = jnp.zeros_like(hr[turn, 0])

    @pl.when(tr == n_tr - 1)
    def _():
        for turn in range(2):
            hr[turn, 1] = jnp.zeros_like(hr[turn, 1])

    @pl.when(los == 0)
    def _():
        for turn in range(2):
            cr[turn, 0] = jnp.zeros_like(cr[turn, 0])

    @pl.when(los == n_los - 1)
    def _():
        for turn in range(2):
            cr[turn, 1] = jnp.zeros_like(cr[turn, 1])

    barrier = pltpu.get_barrier_semaphore()
    for slot in range(1, n_tr):
        pl.semaphore_signal(barrier, inc=1, device_id=(tr_peer(slot), los), device_id_type=MESH)
    for step in range(1, n_los):
        pl.semaphore_signal(barrier, inc=1, device_id=(tr, los_peer(step)), device_id_type=MESH)

    owner = owner_ref[...]
    hot = jnp.where(iota((n_tr, pix), 0) == owner, 1.0, 0.0).astype(F32)
    blk = min(256, pix)
    blocks = pix // blk
    stacked = jnp.concatenate(
        [hot[:, b * blk:(b + 1) * blk] for b in range(blocks)], axis=0
    ).astype(BF16)
    before = jnp.where(iota((blk, blk), 0) < iota((blk, blk), 1), 1.0, 0.0).astype(BF16)
    prefix = jnp.dot(stacked, before, preferred_element_type=F32)
    carry = jnp.zeros((n_tr, 1), F32)
    ranks = []
    for b in range(blocks):
        part = hot[:, b * blk:(b + 1) * blk]
        ranks.append(
            jnp.sum(part * (prefix[b * n_tr:(b + 1) * n_tr] + carry), axis=0, keepdims=True)
        )
        carry = carry + jnp.sum(part, axis=1, keepdims=True)
    rank = jnp.concatenate(ranks, axis=1).astype(I32)
    slot_hot = jnp.where(iota((CAP, pix), 0) == rank, 1.0, 0.0).astype(BF16)

    weight = weight_ref[...]
    va, vb = two_pieces(jnp.concatenate([flux_ref[...] * weight, weight], axis=0))
    ca, cb = two_pieces(cell_ref[...].astype(F32))
    chans = 2 * planes
    owner16 = jnp.broadcast_to(owner.astype(F32), (chans, pix)).astype(BF16)
    nothing = jnp.zeros((chans, pix), BF16)
    for o in range(n_tr):
        mine = owner16 == jnp.asarray(o, BF16)
        xa[o * chans:(o + 1) * chans, 0:pix] = jnp.where(mine, va, nothing)
        xb[o * chans:(o + 1) * chans, 0:pix] = jnp.where(mine, vb, nothing)
    top = n_tr * chans
    xa[top:top + n_tr, 0:pix] = (hot * ca.astype(F32)).astype(BF16)
    xb[top:top + n_tr, 0:pix] = (hot * cb.astype(F32)).astype(BF16)
    packed = lax.dot_general(xa[0:top + n_tr, 0:pix], slot_hot, NT, preferred_element_type=F32)
    packed = packed + lax.dot_general(xb[0:top + n_tr, 0:pix], slot_hot, NT, preferred_element_type=F32)
    for o in range(n_tr):
        pk[o, 0:chans, :] = packed[o * chans:(o + 1) * chans, :]
        pk[o, chans:chans + 1, :] = packed[top + o:top + o + 1, :]

    pl.semaphore_wait(barrier, n_tr - 1 + n_los - 1)

    routed = []
    for slot in range(n_tr - 1, 0, -1):
        peer = tr_peer(slot)
        copy = send(pk.at[peer], rv.at[slot], route_send.at[slot], route_recv.at[slot], peer, los)
        copy.start()
        routed.append(copy)
    rv[0] = pk[tr]

    def spread(zi, last):
        b = bin_ref[zi]
        kx = jnp.full((8, 128), coef_ref[0, b], F32)
        ky = jnp.full((8, 128), coef_ref[1, b], F32)
        link = jnp.full((8, 128), coef_ref[2, b], F32)
        link = jnp.where(zi < depth - 1, link, jnp.zeros_like(link))
        kxs[zi] = kx
        kys[zi] = ky
        lks[zi] = link
        base[zi] = MASS + 2.0 * kx + 2.0 * ky + (last + link)
        return link

    lax.fori_loop(0, depth, spread, jnp.zeros((8, 128), F32))

    width = n_los * CHUNK
    jump = min(8, n_tr)
    span = jump * CAP
    by_slot = {n_tr - 1 - i: c for i, c in enumerate(routed)}
    for g in range(n_tr // jump):
        slots = range(g * jump, (g + 1) * jump)
        for slot in slots:
            if slot:
                by_slot[slot].wait_recv()
        vals = jnp.concatenate([rv[slot, 0:chans, :] for slot in slots], axis=1)
        cell = jnp.concatenate([rv[slot, chans:chans + 1, :] for slot in slots], axis=1)
        cell = (cell + 0.5).astype(I32)
        col = cell % width
        place = (col // CHUNK) * SX + cell // width
        low = col % CHUNK
        upper = iota((8, span), 0) < SX
        spreads = [
            jnp.where(
                upper,
                jnp.broadcast_to(vals[p:p + 1], (8, span)),
                jnp.broadcast_to(vals[planes + p:planes + p + 1], (8, span)),
            )
            for p in range(planes)
        ]
        ba, bb = two_pieces(jnp.concatenate(spreads, axis=0))
        low_hot = jnp.where(iota((CHUNK, span), 0) == low, 1.0, 0.0).astype(BF16)
        where_to = (
            jnp.broadcast_to(place, (16, span)) - iota((16, span), 0) % SX
        ).astype(F32).astype(BF16)
        none = jnp.zeros((16, span), BF16)
        rows = 8 * planes
        for k in range(n_los):
            mine = where_to == jnp.asarray(SX * k, BF16)
            for t in range(rows // 16):
                at = k * rows + 16 * t
                xa[at:at + 16, 0:span] = jnp.where(mine, ba[16 * t:16 * t + 16], none)
                xb[at:at + 16, 0:span] = jnp.where(mine, bb[16 * t:16 * t + 16], none)
        full = n_los * rows
        part = lax.dot_general(xa[0:full, 0:span], low_hot, NT, preferred_element_type=F32)
        part = part + lax.dot_general(xb[0:full, 0:span], low_hot, NT, preferred_element_type=F32)
        if g == 0:
            acc[...] = part
        else:
            acc[...] = acc[...] + part

    upper3 = iota((planes, 8, 128), 1) < SX
    for k in range(n_los):
        both = acc[k * 8 * planes:(k + 1) * 8 * planes, :]
        left = both[:, 0:128].reshape(planes, 8, 128)
        right = both[:, 128:256].reshape(planes, 8, 128)
        sb[k * planes:(k + 1) * planes, 0] = jnp.where(upper3, left, roll(right, 4, 1))
        sb[k * planes:(k + 1) * planes, 1] = jnp.where(upper3, roll(left, 4, 1), right)
    here = pl.ds(los * planes, planes)
    entered = []
    for step in range(1, n_los):
        peer = los_peer(step)
        copy = send(
            sb.at[pl.ds(peer * planes, planes)], tb.at[here],
            in_send.at[step], in_recv.at[step], tr, peer,
        )
        copy.start()
        entered.append(copy)
    tb[here] = sb[here]
    for copy in entered:
        copy.wait_recv()

    stride = min(8, half)
    zero = jnp.zeros((8, 128), F32)

    def pivots(block, state):
        it, gt, lt, ib, gb = state
        for u in range(stride):
            zt = block * stride + u
            zb = depth - 1 - zt
            it = 1.0 / ((base[zt] + tb[zt, 1]) - (lt * lt) * it)
            gt = (tb[zt, 0] + lt * gt) * it
            lb = lks[zb]
            ib = 1.0 / ((base[zb] + tb[zb, 1]) - (lb * lb) * ib)
            gb = (tb[zb, 0] + lb * gb) * ib
            lt = lks[zt]
            inv[zt] = it
            gf[zt] = gt
            inv[zb] = ib
            gf[zb] = gb
        return it, gt, lt, ib, gb

    it, gt, lt, ib, gb = lax.fori_loop(0, half // stride, pivots, (zero,) * 5)
    ratio_top, ratio_bottom = lt * it, lt * ib
    middle = 1.0 / (1.0 - ratio_top * ratio_bottom)

    def eliminate(block, state):
        gt, lt, gb = state
        for u in range(stride):
            zt = block * stride + u
            zb = depth - 1 - zt
            gt = (qf[zt] + lt * gt) * inv[zt]
            gb = (qf[zb] + lks[zb] * gb) * inv[zb]
            lt = lks[zt]
            gf[zt] = gt
            gf[zb] = gb
        return gt, lt, gb

    def back(out, source, gt, gb):
        yt = (gt + ratio_top * gb) * middle
        yb = gb + ratio_bottom * yt
        out[half - 1] = yt
        out[half] = yb
        total = source(half - 1) * yt + source(half) * yb

        def one(zt, state):
            yt, yb, total = state
            zb = depth - 1 - zt
            yt = gf[zt] + (lks[zt] * inv[zt]) * yt
            yb = gf[zb] + (lks[zb - 1] * inv[zb]) * yb
            out[zt] = yt
            out[zb] = yb
            return yt, yb, total + (source(zt) * yt + source(zb) * yb)

        state = (yt, yb, total)
        for u in range(stride - 1):
            state = one(half - 2 - u, state)

        def some(block, state):
            for u in range(stride):
                state = one(half - 1 - (block * stride + u), state)
            return state

        return lax.fori_loop(1, half // stride, some, state)[2]

    sub = iota((8, 128), 0)
    lane = iota((8, 128), 1)
    quarter = sub % 4
    first_row, last_row = quarter == 0, quarter == 3
    at_left, at_right = lane == 0, lane == 127
    inner_left, inner_right = at_left & (sub >= 4), at_right & (sub < 4)

    def edges(field, turn):
        def rows(i, state):
            left, right = state
            down = up = zero
            for j in range(4):
                zi = i * 4 + j
                v = field[zi]
                down = jnp.where(quarter == j, roll(v, j - 3, 0), down)
                up = jnp.where(quarter == j, roll(v, j, 0), up)
                u = roll(v, 4, 0)
                here_lane = lane == zi
                right = jnp.where(here_lane, roll(u, zi + 1, 1), right)
                left = jnp.where(here_lane, roll(u, zi, 1), left)
            hs[turn, 0, i] = down
            hs[turn, 1, i] = up
            return left, right

        left, right = lax.fori_loop(0, groups, rows, (zero, zero))
        cs[turn, 0] = right
        cs[turn, 1] = left

        def moves(side):
            step = 1 if side == 0 else -1
            last_tr, last_los = (n_tr - 1, n_los - 1) if side == 0 else (0, 0)
            row = send(
                hs.at[turn, side], hr.at[turn, side], halo_send.at[turn, side, 0],
                halo_recv.at[turn, side, 0], (tr + step + n_tr) % n_tr, los,
            )
            column = send(
                cs.at[turn, side], cr.at[turn, side], halo_send.at[turn, side, 1],
                halo_recv.at[turn, side, 1], tr, (los + step + n_los) % n_los,
            )
            return row, column, tr != last_tr, los != last_los

        for side in range(2):
            row, column, has_row, has_column = moves(side)
            pl.when(has_row)(row.start)
            pl.when(has_column)(column.start)
        return [moves(side) for side in range(2)]

    def edges_arrive(moved):
        for side in range(2):
            row, column, has_row, has_column = moved[side]
            pl.when(has_row)(row.wait_send)
            pl.when(has_column)(column.wait_send)
        for side in range(2):
            row, column, _, _ = moved[side]
            first_tr, first_los = (0, 0) if side == 0 else (n_tr - 1, n_los - 1)
            pl.when(tr != first_tr)(row.wait_recv)
            pl.when(los != first_los)(column.wait_recv)

    def operate(field, turn, source, out):
        from_left, from_right = cr[turn, 0], cr[turn, 1]

        def some(i, total):
            above, below = hr[turn, 0, i], hr[turn, 1, i]
            for j in range(4):
                zi = i * 4 + j
                v = field[zi]
                up = jnp.where(first_row, roll(above, -j, 0), roll(v, 1, 0))
                down = jnp.where(last_row, roll(below, 3 - j, 0), roll(v, -1, 0))
                u = roll(v, 4, 0)
                before = jnp.where(at_left, roll(from_left, 128 - zi, 1), roll(v, 1, 1))
                before = jnp.where(inner_left, roll(u, 1, 1), before)
                after = jnp.where(at_right, roll(from_right, 127 - zi, 1), roll(v, 127, 1))
                after = jnp.where(inner_right, roll(u, 127, 1), after)
                image = source(zi) - (kxs[zi] * (up + down) + kys[zi] * (before + after))
                out[zi] = image
                total = total + v * image
            return total

        return lax.fori_loop(0, groups, some, zero)

    def leave(field, which):
        copies = []
        for step in range(1, n_los):
            peer = los_peer(step)
            copy = send(
                field.at[pl.ds(peer * planes, planes)], rb.at[which, los],
                out_send.at[which, step], out_recv.at[which, step], tr, peer,
            )
            copy.start()
            copies.append(copy)
        rb[which, los] = field[here]
        return copies

    right_side = lambda zi: tb[zi, 0]
    image_of = lambda zi: qf[zi]
    dot_bz = back(zf, right_side, gt, gb)
    moved = edges(zf, 0)
    left_z = leave(zf, 0)
    edges_arrive(moved)
    dot_zq = operate(zf, 0, right_side, qf)

    gt, _, gb = lax.fori_loop(0, half // stride, eliminate, (zero,) * 3)
    dot_qw = back(wf, image_of, gt, gb)
    moved = edges(wf, 1)
    left_q = leave(qf, 1)
    left_w = leave(wf, 2)
    edges_arrive(moved)
    dot_ws = operate(wf, 1, image_of, sf)

    for n, dot in enumerate((dot_bz, dot_zq, dot_qw, dot_ws)):
        ps[0, n:n + 1, :] = jnp.sum(dot, axis=0, keepdims=True)
    summed = []
    for slot in range(n_tr - 1, 0, -1):
        copy = send(
            ps.at[0], p1.at[slot], sum_send.at[slot], sum_recv.at[slot], tr_peer(slot), los
        )
        copy.start()
        summed.append(copy)
    left_s = leave(sf, 3)
    total = ps[0]
    for copy in summed:
        copy.wait_recv()
    for slot in range(1, n_tr):
        total = total + p1[slot]
    ps[1] = total
    finals = []
    for step in range(1, n_los):
        copy = send(
            ps.at[1], p2.at[step], fin_send.at[step], fin_recv.at[step], tr, los_peer(step)
        )
        copy.start()
        finals.append(copy)
    for copy in finals:
        copy.wait_recv()
    for step in range(1, n_los):
        total = total + p2[step]
    total = jnp.sum(total, axis=1, keepdims=True)
    bz, zq, qw, ws = (
        jnp.broadcast_to(total[n:n + 1], (8, 128)) for n in range(4)
    )
    alpha = bz / zq
    rz = alpha * alpha * qw - bz
    beta = rz / bz
    grown = 1.0 + beta
    alpha_next = rz / (grown * grown * zq - 2.0 * grown * alpha * qw + alpha * alpha * ws)
    main = alpha + alpha_next * grown
    other = alpha * alpha_next

    for copies in (left_z, left_w, left_q, left_s):
        for copy in copies:
            copy.wait_recv()

    def finish(k, none):
        for p in range(planes):
            x = main * rb[0, k, p] - other * rb[2, k, p]
            r = sb[k * planes + p, 0] - main * rb[1, k, p] + other * rb[3, k, p]
            for part in range(2):
                at = pl.ds(pl.multiple_of(k * CHUNK + part * 128, 128), 128)
                sol_ref[p, :, at] = x[part * SX:(part + 1) * SX]
                res_ref[p, :, at] = r[part * SX:(part + 1) * SX]
        return none

    lax.fori_loop(0, n_los, finish, 0)

    for copies in (routed, entered, left_z, left_q, left_w, left_s, summed, finals):
        for copy in copies:
            copy.wait_send()


def local(flux, noise_weight, pixel_owner, pixel_cell, plane_bin, bin_coeffs):
    n_tr, n_los = lax.axis_size("tr"), lax.axis_size("los")
    nzr = 8 if n_tr == 32 else 2
    planes, pix = flux.shape
    depth = planes * n_los
    cols = n_los * CHUNK
    dma = pltpu.SemaphoreType.DMA
    full = pltpu.VMEM((depth, 8, 128), F32)
    vmem = pl.BlockSpec(memory_space=pltpu.VMEM)
    smem = pl.BlockSpec(memory_space=pltpu.SMEM)
    top = (n_tr * 2 * planes) + n_tr
    out = jax.ShapeDtypeStruct((planes, SX, cols), F32)
    return pl.pallas_call(
        functools.partial(kernel, n_tr, n_los, nzr),
        out_shape=(out, out),
        in_specs=[vmem, vmem, vmem, vmem, smem, smem],
        out_specs=(vmem, vmem),
        scratch_shapes=[
            pltpu.VMEM((max(top, n_los * 8 * planes), max(pix, min(8, n_tr) * CAP)), BF16),
            pltpu.VMEM((max(top, n_los * 8 * planes), max(pix, min(8, n_tr) * CAP)), BF16),
            pltpu.VMEM((n_tr, 2 * planes + 1, CAP), F32),
            pltpu.VMEM((n_tr, 2 * planes + 1, CAP), F32),
            pltpu.VMEM((n_los * 8 * planes, CHUNK), F32),
            pltpu.VMEM((depth, 2, 8, 128), F32),
            pltpu.VMEM((depth, 2, 8, 128), F32),
            full, full, full, full, full, full, full, full, full, full,
            pltpu.VMEM((2, 2, depth // 4, 8, 128), F32),
            pltpu.VMEM((2, 2, depth // 4, 8, 128), F32),
            pltpu.VMEM((2, 2, 8, 128), F32),
            pltpu.VMEM((2, 2, 8, 128), F32),
            pltpu.VMEM((4, n_los, planes, 8, 128), F32),
            pltpu.VMEM((2, 4, 128), F32),
            pltpu.VMEM((n_tr, 4, 128), F32),
            pltpu.VMEM((n_los, 4, 128), F32),
            dma((n_tr,)), dma((n_tr,)), dma((n_los,)), dma((n_los,)),
            dma((2, 2, 2)), dma((2, 2, 2)), dma((4, n_los)), dma((4, n_los)),
            dma((n_tr,)), dma((n_tr,)), dma((n_los,)), dma((n_los,)),
        ],
        compiler_params=pltpu.CompilerParams(
            collective_id=0, has_side_effects=True, vmem_limit_bytes=50 * 1024 * 1024
        ),
        name="wiener",
    )(
        flux, noise_weight, pixel_owner.reshape(1, pix), pixel_cell.reshape(1, pix),
        plane_bin, bin_coeffs,
    )


def solution(mesh):
    placed = (P("los", "tr"), P("los", "tr"), P("tr", None), P("tr"), P(), P())
    return jax.shard_map(
        local,
        mesh=mesh,
        in_specs=placed,
        out_specs=(P("los", "tr", None), P("los", "tr", None)),
        check_vma=False,
    )
```

profile of v0, /device:TPU:1, one launch (start us, length us, event | category | flops | bytes accessed | tf_op | source)
XLA Modules:
  0.0 63.6 jit_solution(17137163816270441815)
XLA Ops:
  0.6 0.0 copy-start.4
  0.6 0.0 copy-start.5
  0.7 0.7 %copy-done.4 = f32[3,8]{1,0:T(4,128)S(1)} copy-done((f32[3,8]{1,0:T(4,128)S(1)}, f32[3,8]{1,0:T(4,128)}, u32[]{:S(2)}) %copy-start.4) | copy-done | bytes 120
  1.3 0.0 copy-done.5
  1.3 0.0 copy-start
  1.3 0.8 %copy-done = f32[8,2048]{1,0:T(8,128)S(1)} copy-done((f32[8,2048]{1,0:T(8,128)S(1)}, f32[8,2048]{1,0:T(8,128)}, u32[]{:S(2)}) %copy-start) | copy-done | bytes 65560
  2.2 0.0 copy-start.1
  2.2 0.8 %copy-done.1 = f32[8,2048]{1,0:T(8,128)S(1)} copy-done((f32[8,2048]{1,0:T(8,128)S(1)}, f32[8,2048]{1,0:T(8,128)}, u32[]{:S(2)}) %copy-start.1) | copy-done | bytes 65560
  3.0 0.0 copy-start.2
  3.0 0.7 %copy-done.2 = s32[2048,1]{0,1:T(1,128)S(1)} copy-done((s32[2048,1]{0,1:T(1,128)S(1)}, s32[2048,1]{0,1:T(1,128)}, u32[]{:S(2)}) %copy-start.2) | copy-done | bytes 8216
  3.7 0.0 copy-start.3
  3.7 0.7 %copy-done.3 = s32[2048]{0:T(1024)S(1)} copy-done((s32[2048]{0:T(1024)S(1)}, s32[2048]{0:T(1024)}, u32[]{:S(2)}) %copy-start.3) | copy-done | bytes 8216
  4.4 57.8 %wiener.1 = (f32[8,4,2048]{2,1,0:T(4,128)S(1)}, f32[8,4,2048]{2,1,0:T(4,128)S(1)}) custom-call(f32[8,2048]{1,0:T(8,128)S(1)} %copy-done, f32[8,2048]{1,0:T(8,128)S(1)} %copy-done.1, s32[1,2048]{1,0:T(1,128)S(1)} %bitcast.2, s32[1,2048]{1,0:T(1,128)S(1)} %bitcast.3, s32[64]{0:T(128)S(1)} %copy-done.5, f32[3,8]{1,0:T(4,128)S(1)} %copy-done.4), custom_call_target="tpu_custom_call" | custom-call | tf_op jit(solution)/shard_map/wiener/pallas_call | solution.py:466
  62.2 0.7 %copy.10 = f32[8,4,2048]{2,1,0:T(4,128)} copy(f32[8,4,2048]{2,1,0:T(4,128)S(1)} %get-tuple-element.4) | data formatting | bytes 524288
  62.9 0.7 %copy.11 = f32[8,4,2048]{2,1,0:T(4,128)} copy(f32[8,4,2048]{2,1,0:T(4,128)S(1)} %get-tuple-element.5) | data formatting | bytes 524288
Async XLA Ops:
  0.6 0.7 %copy-start.4 = (f32[3,8]{1,0:T(4,128)S(1)}, f32[3,8]{1,0:T(4,128)}, u32[]{:S(2)}) copy-start(f32[3,8]{1,0:T(4,128)} %coef_ref.1) | copy-start | bytes 292
  0.6 0.7 %copy-start.5 = (s32[64]{0:T(128)S(1)}, s32[64]{0:T(128)}, u32[]{:S(2)}) copy-start(s32[64]{0:T(128)} %bin_ref.1) | copy-start | bytes 772
  1.3 0.8 %copy-start = (f32[8,2048]{1,0:T(8,128)S(1)}, f32[8,2048]{1,0:T(8,128)}, u32[]{:S(2)}) copy-start(f32[8,2048]{1,0:T(8,128)} %flux_ref.1) | copy-start | bytes 196612
  2.2 0.8 %copy-start.1 = (f32[8,2048]{1,0:T(8,128)S(1)}, f32[8,2048]{1,0:T(8,128)}, u32[]{:S(2)}) copy-start(f32[8,2048]{1,0:T(8,128)} %weight_ref.1) | copy-start | bytes 196612
  3.0 0.7 %copy-start.2 = (s32[2048,1]{0,1:T(1,128)S(1)}, s32[2048,1]{0,1:T(1,128)}, u32[]{:S(2)}) copy-start(s32[2048,1]{0,1:T(1,128)} %param.8) | copy-start | bytes 24580
  3.7 0.7 %copy-start.3 = (s32[2048]{0:T(1024)S(1)}, s32[2048]{0:T(1024)}, u32[]{:S(2)}) copy-start(s32[2048]{0:T(1024)} %param.9) | copy-start | bytes 24580
where the time goes:
time: 63.9 us; the launch traced here: 63.6 us
  Pallas kernels  57.8 us (90%)
  local copies, waits for them, and re-layouts  5.15 us (8%)
  between operations  0.66 us (1%)
    pallas_call x1, Pallas kernels, local(): pl.pallas_call(functools.partial(kernel, n_tr, n_los, nzr), out_shape=(ou...  57.8 us
    unnamed x14, local copies, waits for them, and re-layouts  5.15 us

commit v1 on v0

v1 whole, which is shorter than its diff:
```python
import functools

import jax
import jax.numpy as jnp
from jax import lax
from jax.experimental import pallas as pl
from jax.experimental.pallas import tpu as pltpu
from jax.sharding import PartitionSpec as P

MESH = pl.DeviceIdType.MESH
F32 = jnp.float32
BF16 = jnp.bfloat16
I32 = jnp.int32
SX = 4
CHUNK = 256
CAP = 128
MASS = 0.5
NT = (((1,), (1,)), ((), ()))


def iota(shape, dim):
    return lax.broadcasted_iota(I32, shape, dim)


def two_pieces(values):
    high = values.astype(BF16)
    return high, (values - high.astype(F32)).astype(BF16)


def roll(x, shift, axis):
    size = x.shape[axis]
    return pltpu.roll(x, shift % size if isinstance(shift, int) else shift, axis)


def kernel(
    n_tr, n_los, nzr, flux_hbm, weight_hbm, owner_hbm, cell_hbm, bin_hbm, coef_hbm,
    sol_ref, res_ref,
    flux_ref, weight_ref, owner_ref, cell_ref, bin_ref, coef_ref,
    xp, xs, pw, pf, rw, rf, lows, dests, acc, sw, sf, tw, tf,
    kxs, kys, lks, base, inv, gf, zf, qf, wf, vf, pre,
    hs, hr, cs, cr, rb, ps, p1, p2,
    load_sem, route_send, route_recv, in_send, in_recv, halo_send, halo_recv,
    out_send, out_recv, sum_send, sum_recv, fin_send, fin_recv,
):
    planes, pix = flux_ref.shape
    depth = planes * n_los
    half = depth // 2
    groups = depth // 4
    tr = lax.axis_index("tr")
    los = lax.axis_index("los")
    nyr = n_tr // nzr
    y, zc = tr // nzr, tr % nzr
    offsets = [(dy, dz) for dy in range(nyr) for dz in range(nzr)]
    offsets.sort(key=lambda o: (min(o[0], nyr - o[0]) + min(o[1], nzr - o[1]), o))
    far_steps = sorted(range(1, n_los), key=lambda d: -min(d, n_los - d))

    def tr_peer(slot):
        dy, dz = offsets[slot]
        return ((y + dy) % nyr) * nzr + (zc + dz) % nzr

    def los_peer(step):
        return (los + step) % n_los

    def send(src, dst, ssem, rsem, at_tr, at_los):
        return pltpu.make_async_remote_copy(
            src_ref=src, dst_ref=dst, send_sem=ssem, recv_sem=rsem,
            device_id=(at_tr, at_los), device_id_type=MESH,
        )

    loads = [
        pltpu.make_async_copy(src, dst, load_sem.at[n])
        for n, (src, dst) in enumerate((
            (owner_hbm, owner_ref), (weight_hbm, weight_ref), (cell_hbm, cell_ref),
            (flux_hbm, flux_ref), (bin_hbm, bin_ref), (coef_hbm, coef_ref),
        ))
    ]
    for load in loads:
        load.start()

    @pl.when(tr == 0)
    def _():
        for turn in range(2):
            hr[turn, 0] = jnp.zeros_like(hr[turn, 0])

    @pl.when(tr == n_tr - 1)
    def _():
        for turn in range(2):
            hr[turn, 1] = jnp.zeros_like(hr[turn, 1])

    @pl.when(los == 0)
    def _():
        for turn in range(2):
            cr[turn, 0] = jnp.zeros_like(cr[turn, 0])

    @pl.when(los == n_los - 1)
    def _():
        for turn in range(2):
            cr[turn, 1] = jnp.zeros_like(cr[turn, 1])

    barrier = pltpu.get_barrier_semaphore()
    for slot in range(n_tr - 1, 0, -1):
        pl.semaphore_signal(barrier, inc=1, device_id=(tr_peer(slot), los), device_id_type=MESH)
    for step in far_steps:
        pl.semaphore_signal(barrier, inc=1, device_id=(tr, los_peer(step)), device_id_type=MESH)

    loads[0].wait()
    owner = owner_ref[...]
    hot = jnp.where(iota((n_tr, pix), 0) == owner, 1.0, 0.0).astype(F32)
    blk = min(256, pix)
    blocks = pix // blk
    stacked = jnp.concatenate(
        [hot[:, b * blk:(b + 1) * blk] for b in range(blocks)], axis=0
    ).astype(BF16)
    before = jnp.where(iota((blk, blk), 0) < iota((blk, blk), 1), 1.0, 0.0).astype(BF16)
    prefix = jnp.dot(stacked, before, preferred_element_type=F32)
    carry = jnp.zeros((n_tr, 1), F32)
    ranks = []
    for b in range(blocks):
        part = hot[:, b * blk:(b + 1) * blk]
        ranks.append(
            jnp.sum(part * (prefix[b * n_tr:(b + 1) * n_tr] + carry), axis=0, keepdims=True)
        )
        carry = carry + jnp.sum(part, axis=1, keepdims=True)
    rank = jnp.concatenate(ranks, axis=1).astype(I32)
    slot_hot = jnp.where(iota((CAP, pix), 0) == rank, 1.0, 0.0).astype(BF16)
    pair = 16 // planes
    owner16 = (
        jnp.broadcast_to(owner, (16, pix)) - iota((16, pix), 0) // planes
    ).astype(F32).astype(BF16)
    nothing = jnp.zeros((16, pix), BF16)
    rows = n_tr * planes

    def spread_by_owner(values, at):
        twice = jnp.concatenate([values] * pair, axis=0)
        for o in range(0, n_tr, pair):
            xp[at + o * planes:at + (o + pair) * planes, :] = jnp.where(
                owner16 == jnp.asarray(o, BF16), twice, nothing
            )

    for load in loads[1:]:
        load.wait()
    weight = weight_ref[...]
    wa, wb = two_pieces(weight)
    ca, cb = two_pieces(cell_ref[...].astype(F32))
    extra = rows + n_tr
    spread_by_owner(wa, 0)
    spread_by_owner(wb, extra)
    xp[rows:extra, :] = (hot * ca.astype(F32)).astype(BF16)
    xp[extra + rows:2 * extra, :] = (hot * cb.astype(F32)).astype(BF16)
    packed = lax.dot_general(xp[...], slot_hot, NT, preferred_element_type=F32)
    packed = packed[0:extra] + packed[extra:2 * extra]
    for o in range(n_tr):
        pw[o, 0:planes, :] = packed[o * planes:(o + 1) * planes]
        pw[o, planes:planes + 1, :] = packed[rows + o:rows + o + 1]

    pl.semaphore_wait(barrier, n_tr - 1 + n_los - 1)

    routed = [None], [None]

    def route(stage, packs, into):
        for slot in range(1, n_tr):
            peer = tr_peer(slot)
            routed[stage].append(send(
                packs.at[peer], into.at[slot],
                route_send.at[stage, slot], route_recv.at[stage, slot], peer, los,
            ))
        for copy in routed[stage][:0:-1]:
            copy.start()

    route(0, pw, rw)
    rw[0] = pw[tr]

    fa, fb = two_pieces(flux_ref[...] * weight)
    spread_by_owner(fa, 0)
    spread_by_owner(fb, rows)
    packed = lax.dot_general(xp[0:2 * rows, :], slot_hot, NT, preferred_element_type=F32)
    packed = packed[0:rows] + packed[rows:2 * rows]
    for o in range(n_tr):
        pf[o] = packed[o * planes:(o + 1) * planes]
    route(1, pf, rf)
    rf[0] = pf[tr]

    def spread(zi, last):
        b = bin_ref[zi]
        kx = jnp.full((8, 128), coef_ref[0, b], F32)
        ky = jnp.full((8, 128), coef_ref[1, b], F32)
        link = jnp.full((8, 128), coef_ref[2, b], F32)
        link = jnp.where(zi < depth - 1, link, jnp.zeros_like(link))
        kxs[zi] = kx
        kys[zi] = ky
        lks[zi] = link
        base[zi] = MASS + 2.0 * kx + 2.0 * ky + (last + link)
        return link

    lax.fori_loop(0, depth, spread, jnp.zeros((8, 128), F32))

    width = n_los * CHUNK
    jump = min(8, n_tr)
    span = jump * CAP
    chunks = n_tr // jump
    each = SX * planes
    full = n_los * each
    upper = iota((8, span), 0) < SX
    low_iota = iota((CHUNK, span), 0)
    row16 = iota((16, span), 0) % SX
    none = jnp.zeros((16, span), BF16)
    upper3 = iota((planes // 2, 8, 128), 1) < SX

    def scatter(stage, arrived):
        for g in range(chunks - 1, -1, -1):
            slots = range(g * jump, (g + 1) * jump)
            for slot in reversed(slots):
                if slot:
                    routed[stage][slot].wait_recv()
            if stage == 0:
                cell = jnp.concatenate([arrived[t, planes:planes + 1, :] for t in slots], axis=1)
                cell = (cell + 0.5).astype(I32)
                col = cell % width
                place = (col // CHUNK) * SX + cell // width
                low = jnp.broadcast_to(col % CHUNK, (CHUNK, span))
                lows[g] = jnp.where(low_iota == low, 1.0, 0.0).astype(BF16)
                dests[g] = (
                    jnp.broadcast_to(place, (16, span)) - row16
                ).astype(F32).astype(BF16)
            vals = jnp.concatenate([arrived[t, 0:planes, :] for t in slots], axis=1)
            ba, bb = two_pieces(jnp.concatenate([
                jnp.where(
                    upper,
                    jnp.broadcast_to(vals[p:p + 1], (8, span)),
                    jnp.broadcast_to(vals[p + 1:p + 2], (8, span)),
                )
                for p in range(0, planes, 2)
            ], axis=0))
            dest = dests[g]
            for k in range(n_los):
                mine = dest == jnp.asarray(SX * k, BF16)
                for t in range(0, each, 16):
                    at = k * each + t
                    xs[at:at + 16, :] = jnp.where(mine, ba[t:t + 16], none)
                    xs[full + at:full + at + 16, :] = jnp.where(mine, bb[t:t + 16], none)
            part = lax.dot_general(xs[...], lows[g], NT, preferred_element_type=F32)
            part = part[0:full] + part[full:2 * full]
            if g == chunks - 1:
                acc[...] = part
            else:
                acc[...] = acc[...] + part

    here = pl.ds(los * planes, planes)

    def enter(stage, out, into):
        for k in range(n_los):
            both = acc[k * each:(k + 1) * each, :]
            left = both[:, 0:128].reshape(planes // 2, 8, 128)
            right = both[:, 128:256].reshape(planes // 2, 8, 128)
            even = jnp.where(upper3, left, roll(right, 4, 1))
            odd = jnp.where(upper3, roll(left, 4, 1), right)
            for p in range(planes // 2):
                out[k * planes + 2 * p] = even[p]
                out[k * planes + 2 * p + 1] = odd[p]
        copies = []
        for step in far_steps:
            peer = los_peer(step)
            copy = send(
                out.at[pl.ds(peer * planes, planes)], into.at[here],
                in_send.at[stage, step], in_recv.at[stage, step], tr, peer,
            )
            copy.start()
            copies.append(copy)
        into[here] = out[here]
        return copies

    scatter(0, rw)
    entered_w = enter(0, sw, tw)
    scatter(1, rf)
    entered_f = enter(1, sf, tf)

    for copy in entered_w:
        copy.wait_recv()

    stride = min(8, half)
    zero = jnp.zeros((8, 128), F32)

    def pivots(block, state):
        it, lt, ib = state
        for u in range(stride):
            zt = block * stride + u
            zb = depth - 1 - zt
            it = 1.0 / ((base[zt] + tw[zt]) - (lt * lt) * it)
            lb = lks[zb]
            ib = 1.0 / ((base[zb] + tw[zb]) - (lb * lb) * ib)
            lt = lks[zt]
            inv[zt] = it
            inv[zb] = ib
        return it, lt, ib

    it, lt, ib = lax.fori_loop(0, half // stride, pivots, (zero,) * 3)
    ratio_top, ratio_bottom = lt * it, lt * ib
    middle = 1.0 / (1.0 - ratio_top * ratio_bottom)

    def solve(source, out):
        def eliminate(block, state):
            gt, lt, gb = state
            for u in range(stride):
                zt = block * stride + u
                zb = depth - 1 - zt
                gt = (source[zt] + lt * gt) * inv[zt]
                gb = (source[zb] + lks[zb] * gb) * inv[zb]
                lt = lks[zt]
                gf[zt] = gt
                gf[zb] = gb
            return gt, lt, gb

        gt, _, gb = lax.fori_loop(0, half // stride, eliminate, (zero,) * 3)
        yt = (gt + ratio_top * gb) * middle
        yb = gb + ratio_bottom * yt
        out[half - 1] = yt
        out[half] = yb
        total = source[half - 1] * yt + source[half] * yb

        def one(zt, state):
            yt, yb, total = state
            zb = depth - 1 - zt
            yt = gf[zt] + (lks[zt] * inv[zt]) * yt
            yb = gf[zb] + (lks[zb - 1] * inv[zb]) * yb
            out[zt] = yt
            out[zb] = yb
            return yt, yb, total + (source[zt] * yt + source[zb] * yb)

        state = (yt, yb, total)
        for u in range(stride - 1):
            state = one(half - 2 - u, state)

        def some(block, state):
            for u in range(stride):
                state = one(half - 1 - (block * stride + u), state)
            return state

        return lax.fori_loop(1, half // stride, some, state)[2]

    sub = iota((8, 128), 0)
    lane = iota((8, 128), 1)
    quarter = sub % 4
    first_row, last_row = quarter == 0, quarter == 3
    in_half = sub < 4
    inner_left, inner_right = (lane == 0) & ~in_half, (lane == 127) & in_half
    outer = ((lane == 0) & in_half) | ((lane == 127) & ~in_half)

    def edge_copy(turn, side, kind):
        step = 1 if side == 0 else -1
        if kind == 0:
            src, dst, where = hs.at[turn, side], hr.at[turn, side], (
                (tr + step + n_tr) % n_tr, los)
        else:
            src, dst, where = cs.at[turn], cr.at[turn, side], (tr, (los + step + n_los) % n_los)
        return send(
            src, dst, halo_send.at[turn, side, kind], halo_recv.at[turn, side, kind], *where
        )

    def edge_each(turn, kind, what):
        for side in range(2):
            copy = edge_copy(turn, side, kind)
            here_is, size = (tr, n_tr) if kind == 0 else (los, n_los)
            first, last = (0, size - 1) if side == 0 else (size - 1, 0)
            if what == "start":
                pl.when(here_is != last)(copy.start)
            elif what == "sent":
                pl.when(here_is != last)(copy.wait_send)
            else:
                pl.when(here_is != first)(copy.wait_recv)

    wide = 8

    def edge_rows(field, turn):
        def pack(block, none):
            for i in range(2):
                down = up = zero
                for j in range(4):
                    v = field[block * wide + i * 4 + j]
                    down = jnp.where(quarter == j, roll(v, j - 3, 0), down)
                    up = jnp.where(quarter == j, roll(v, j, 0), up)
                hs[turn, 0, block * 2 + i] = down
                hs[turn, 1, block * 2 + i] = up
            return none

        lax.fori_loop(0, depth // wide, pack, 0)
        edge_each(turn, 0, "start")

    def edge_columns(field, turn):
        def pack(block, found):
            for i in range(wide):
                zi = block * wide + i
                u = roll(field[zi], 4, 0)
                both = jnp.where(in_half, roll(u, 1, 1), u)
                found = jnp.where(lane == zi, roll(both, zi, 1), found)
            return found

        cs[turn] = lax.fori_loop(0, depth // wide, pack, zero)
        edge_each(turn, 1, "start")

    def operate_inside(field, source):
        def some(block, none):
            for i in range(wide):
                zi = block * wide + i
                v = field[zi]
                u = roll(v, 4, 0)
                up = jnp.where(first_row, 0.0, roll(v, 1, 0))
                down = jnp.where(last_row, 0.0, roll(v, -1, 0))
                before = jnp.where(inner_left, roll(u, 1, 1), roll(v, 1, 1))
                after = jnp.where(inner_right, roll(u, 127, 1), roll(v, 127, 1))
                beside = jnp.where(in_half & (lane == 0), after, before + after)
                beside = jnp.where((lane == 127) & ~in_half, before, beside)
                pre[zi] = source[zi] - (kxs[zi] * (up + down) + kys[zi] * beside)
            return none

        lax.fori_loop(0, depth // wide, some, 0)

    def operate_edges(field, turn, out):
        columns = jnp.where(in_half, cr[turn, 0], roll(cr[turn, 1], 127, 1))

        def some(block, total):
            for i in range(wide):
                zi = block * wide + i
                j = i % 4
                above, below = hr[turn, 0, block * 2 + i // 4], hr[turn, 1, block * 2 + i // 4]
                rows = jnp.where(
                    first_row, roll(above, -j, 0), jnp.where(last_row, roll(below, 3 - j, 0), 0.0)
                )
                beside = jnp.where(outer, roll(columns, 128 - zi, 1), 0.0)
                image = pre[zi] - (kxs[zi] * rows + kys[zi] * beside)
                out[zi] = image
                total = total + field[zi] * image
            return total

        return lax.fori_loop(0, depth // wide, some, zero)

    def leave(field, which):
        copies = []
        for step in far_steps:
            peer = los_peer(step)
            copy = send(
                field.at[pl.ds(peer * planes, planes)], rb.at[which, los],
                out_send.at[which, step], out_recv.at[which, step], tr, peer,
            )
            copy.start()
            copies.append(copy)
        rb[which, los] = field[here]
        return copies

    for copy in entered_f:
        copy.wait_recv()
    dot_bz = solve(tf, zf)
    edge_rows(zf, 0)
    edge_columns(zf, 0)
    left_z = leave(zf, 0)
    operate_inside(zf, tf)
    edge_each(0, 0, "arrived")
    edge_each(0, 1, "arrived")
    dot_zq = operate_edges(zf, 0, qf)
    dot_qw = solve(qf, wf)
    edge_rows(wf, 1)
    edge_columns(wf, 1)
    left_q = leave(qf, 1)
    left_w = leave(wf, 2)
    operate_inside(wf, qf)
    edge_each(1, 0, "arrived")
    edge_each(1, 1, "arrived")
    dot_ws = operate_edges(wf, 1, vf)

    for n, dot in enumerate((dot_bz, dot_zq, dot_qw, dot_ws)):
        ps[0, n:n + 1, :] = jnp.sum(dot, axis=0, keepdims=True)
    summed = []
    for slot in range(n_tr - 1, 0, -1):
        copy = send(
            ps.at[0], p1.at[slot], sum_send.at[slot], sum_recv.at[slot], tr_peer(slot), los
        )
        copy.start()
        summed.append(copy)
    left_v = leave(vf, 3)
    total = ps[0]
    for copy in summed:
        copy.wait_recv()
    for slot in range(1, n_tr):
        total = total + p1[slot]
    ps[1] = total
    finals = []
    for step in far_steps:
        copy = send(
            ps.at[1], p2.at[step], fin_send.at[step], fin_recv.at[step], tr, los_peer(step)
        )
        copy.start()
        finals.append(copy)
    for copy in finals:
        copy.wait_recv()
    for step in range(1, n_los):
        total = total + p2[step]
    total = jnp.sum(total, axis=1, keepdims=True)
    bz, zq, qw, ws = (
        jnp.broadcast_to(total[n:n + 1], (8, 128)) for n in range(4)
    )
    alpha = bz / zq
    rz = alpha * alpha * qw - bz
    beta = rz / bz
    grown = 1.0 + beta
    alpha_next = rz / (grown * grown * zq - 2.0 * grown * alpha * qw + alpha * alpha * ws)
    main = alpha + alpha_next * grown
    other = alpha * alpha_next

    for copies in (left_z, left_w, left_q, left_v):
        for copy in copies:
            copy.wait_recv()

    def finish(k, none):
        for p in range(planes):
            x = main * rb[0, k, p] - other * rb[2, k, p]
            r = sf[k * planes + p] - main * rb[1, k, p] + other * rb[3, k, p]
            for part in range(2):
                at = pl.ds(pl.multiple_of(k * CHUNK + part * 128, 128), 128)
                sol_ref[p, :, at] = x[part * SX:(part + 1) * SX]
                res_ref[p, :, at] = r[part * SX:(part + 1) * SX]
        return none

    lax.fori_loop(0, n_los, finish, 0)

    for copies in (routed[0][1:], routed[1][1:], entered_w, entered_f,
                   left_z, left_q, left_w, left_v, summed, finals):
        for copy in copies:
            copy.wait_send()
    for turn in range(2):
        for kind in range(2):
            edge_each(turn, kind, "sent")


def local(flux, noise_weight, pixel_owner, pixel_cell, plane_bin, bin_coeffs):
    n_tr, n_los = lax.axis_size("tr"), lax.axis_size("los")
    nzr = 8 if n_tr == 32 else 2
    planes, pix = flux.shape
    depth = planes * n_los
    cols = n_los * CHUNK
    jump = min(8, n_tr)
    span = jump * CAP
    each = SX * planes
    dma = pltpu.SemaphoreType.DMA
    field = pltpu.VMEM((depth, 8, 128), F32)
    vmem = pl.BlockSpec(memory_space=pltpu.VMEM)
    hbm = pl.BlockSpec(memory_space=pltpu.MemorySpace.HBM)
    out = jax.ShapeDtypeStruct((planes, SX, cols), F32)
    return pl.pallas_call(
        functools.partial(kernel, n_tr, n_los, nzr),
        out_shape=(out, out),
        in_specs=[hbm] * 6,
        out_specs=(vmem, vmem),
        scratch_shapes=[
            pltpu.VMEM((planes, pix), F32), pltpu.VMEM((planes, pix), F32),
            pltpu.VMEM((1, pix), I32), pltpu.VMEM((1, pix), I32),
            pltpu.SMEM(plane_bin.shape, I32), pltpu.SMEM(bin_coeffs.shape, F32),
            pltpu.VMEM((2 * n_tr * (planes + 1), pix), BF16),
            pltpu.VMEM((2 * n_los * each, span), BF16),
            pltpu.VMEM((n_tr, planes + 1, CAP), F32),
            pltpu.VMEM((n_tr, planes, CAP), F32),
            pltpu.VMEM((n_tr, planes + 1, CAP), F32),
            pltpu.VMEM((n_tr, planes, CAP), F32),
            pltpu.VMEM((n_tr // jump, CHUNK, span), BF16),
            pltpu.VMEM((n_tr // jump, 16, span), BF16),
            pltpu.VMEM((n_los * each, CHUNK), F32),
            field, field, field, field,
            field, field, field, field, field, field, field, field, field, field, field,
            pltpu.VMEM((2, 2, depth // 4, 8, 128), F32),
            pltpu.VMEM((2, 2, depth // 4, 8, 128), F32),
            pltpu.VMEM((2, 8, 128), F32),
            pltpu.VMEM((2, 2, 8, 128), F32),
            pltpu.VMEM((4, n_los, planes, 8, 128), F32),
            pltpu.VMEM((2, 4, 128), F32),
            pltpu.VMEM((n_tr, 4, 128), F32),
            pltpu.VMEM((n_los, 4, 128), F32),
            dma((6,)), dma((2, n_tr)), dma((2, n_tr)), dma((2, n_los)), dma((2, n_los)),
            dma((2, 2, 2)), dma((2, 2, 2)), dma((4, n_los)), dma((4, n_los)),
            dma((n_tr,)), dma((n_tr,)), dma((n_los,)), dma((n_los,)),
        ],
        compiler_params=pltpu.CompilerParams(
            collective_id=0, has_side_effects=True, vmem_limit_bytes=50 * 1024 * 1024
        ),
        name="wiener",
    )(
        *(pltpu.with_memory_space_constraint(x, pltpu.MemorySpace.HBM) for x in (
            flux, noise_weight, pixel_owner.reshape(1, pix), pixel_cell.reshape(1, pix),
            plane_bin, bin_coeffs,
        ))
    )


def solution(mesh):
    placed = (P("los", "tr"), P("los", "tr"), P("tr", None), P("tr"), P(), P())
    return jax.shard_map(
        local,
        mesh=mesh,
        in_specs=placed,
        out_specs=(P("los", "tr", None), P("los", "tr", None)),
        check_vma=False,
    )
```

time: 63.9 us -> 52.6 us (0.82)
  Pallas kernels: 57.8 us -> 50.4 us
  local copies, waits for them, and re-layouts: 5.15 us -> 1.41 us
    pallas_call x1, Pallas kernels: 57.8 us -> 50.4 us  [local(): pl.pallas_call(functools.partial(kernel, n_tr, n_los, nzr), out_shape=(ou...]
    unnamed x14 -> x2, local copies, waits for them, and re-layouts: 5.15 us -> 1.41 us
where the time goes in v1:
time: 52.6 us; the launch traced here: 52.5 us
  Pallas kernels  50.4 us (96%)
  local copies, waits for them, and re-layouts  1.41 us (3%)
  between operations  0.64 us (1%)
    pallas_call x1, Pallas kernels, local(): pl.pallas_call(functools.partial(kernel, n_tr, n_los, nzr), out_shape=(ou...  50.4 us
    unnamed x2, local copies, waits for them, and re-layouts  1.41 us

profile of v1, /device:TPU:1, one launch (start us, length us, event | category | flops | bytes accessed | tf_op | source)
XLA Modules:
  0.0 52.5 jit_solution(17405289364675973695)
XLA Ops:
  0.6 50.4 %wiener.1 = (f32[8,4,2048]{2,1,0:T(4,128)S(1)}, f32[8,4,2048]{2,1,0:T(4,128)S(1)}) custom-call(f32[8,2048]{1,0:T(8,128)} %flux_hbm.1, f32[8,2048]{1,0:T(8,128)} %weight_hbm.1, s32[1,2048]{1,0:T(1,128)} %bitcast.2, s32[1,2048]{1,0:T(1,128)} %bitcast.3, s32[64]{0:T(128)} %bin_hbm.1, f32[3,8]{1,0:T(4,128)} %coef_hbm.1), custom_call_target="tpu_custom_call" | custom-call | tf_op jit(solution)/shard_map/wiener/pallas_call | solution.py:547
  51.1 0.7 %copy.10 = f32[8,4,2048]{2,1,0:T(4,128)} copy(f32[8,4,2048]{2,1,0:T(4,128)S(1)} %get-tuple-element.4) | data formatting | bytes 524288
  51.8 0.7 %copy.11 = f32[8,4,2048]{2,1,0:T(4,128)} copy(f32[8,4,2048]{2,1,0:T(4,128)S(1)} %get-tuple-element.5) | data formatting | bytes 524288

commit v2 on v1

--- a/solution.py
+++ b/solution.py
@@ -36,7 +36,7 @@
     n_tr, n_los, nzr, flux_hbm, weight_hbm, owner_hbm, cell_hbm, bin_hbm, coef_hbm,
     sol_ref, res_ref,
     flux_ref, weight_ref, owner_ref, cell_ref, bin_ref, coef_ref,
-    xp, xs, pw, pf, rw, rf, lows, dests, acc, sw, sf, tw, tf,
+    xp, hot_slot, xs, pw, pf, rw, rf, lows, dests, acc, sw, sf, tw, tf,
     kxs, kys, lks, base, inv, gf, zf, qf, wf, vf, pre,
     hs, hr, cs, cr, rb, ps, p1, p2,
     load_sem, route_send, route_recv, in_send, in_recv, halo_send, halo_recv,
@@ -54,18 +54,28 @@
     offsets.sort(key=lambda o: (min(o[0], nyr - o[0]) + min(o[1], nzr - o[1]), o))
     far_steps = sorted(range(1, n_los), key=lambda d: -min(d, n_los - d))
 
+    ring_y = [((y + d) % nyr) * nzr for d in range(nyr)]
+    ring_z = [(zc + d) % nzr for d in range(nzr)]
+    ring_los = [(los + d) % n_los for d in range(n_los)]
+
     def tr_peer(slot):
         dy, dz = offsets[slot]
-        return ((y + dy) % nyr) * nzr + (zc + dz) % nzr
+        return ring_y[dy] + ring_z[dz]
 
     def los_peer(step):
-        return (los + step) % n_los
+        return ring_los[step]
 
     def send(src, dst, ssem, rsem, at_tr, at_los):
         return pltpu.make_async_remote_copy(
             src_ref=src, dst_ref=dst, send_sem=ssem, recv_sem=rsem,
             device_id=(at_tr, at_los), device_id_type=MESH,
         )
+
+    barrier = pltpu.get_barrier_semaphore()
+    for slot in range(n_tr - 1, 0, -1):
+        pl.semaphore_signal(barrier, inc=1, device_id=(tr_peer(slot), los), device_id_type=MESH)
+    for step in far_steps:
+        pl.semaphore_signal(barrier, inc=1, device_id=(tr, los_peer(step)), device_id_type=MESH)
 
     loads = [
         pltpu.make_async_copy(src, dst, load_sem.at[n])
@@ -96,12 +106,6 @@
     def _():
         for turn in range(2):
             cr[turn, 1] = jnp.zeros_like(cr[turn, 1])
-
-    barrier = pltpu.get_barrier_semaphore()
-    for slot in range(n_tr - 1, 0, -1):
-        pl.semaphore_signal(barrier, inc=1, device_id=(tr_peer(slot), los), device_id_type=MESH)
-    for step in far_steps:
-        pl.semaphore_signal(barrier, inc=1, device_id=(tr, los_peer(step)), device_id_type=MESH)
 
     loads[0].wait()
     owner = owner_ref[...]
@@ -121,41 +125,61 @@
             jnp.sum(part * (prefix[b * n_tr:(b + 1) * n_tr] + carry), axis=0, keepdims=True)
         )
         carry = carry + jnp.sum(part, axis=1, keepdims=True)
-    rank = jnp.concatenate(ranks, axis=1).astype(I32)
-    slot_hot = jnp.where(iota((CAP, pix), 0) == rank, 1.0, 0.0).astype(BF16)
+    rank = jnp.concatenate(ranks, axis=1)
+    which = owner // 2
+    one = jnp.ones((16, pix), BF16)
+    nothing = jnp.zeros((16, pix), BF16)
+    sub16 = iota((16, pix), 0)
+    lanes = (
+        jnp.broadcast_to(rank.astype(I32) + CAP * (owner - 2 * which), (16, pix)) - sub16
+    ).astype(F32).astype(BF16)
+    for t in range(0, 2 * CAP, 16):
+        hot_slot[t:t + 16, :] = jnp.where(lanes == jnp.asarray(t, BF16), one, nothing)
     pair = 16 // planes
-    owner16 = (
-        jnp.broadcast_to(owner, (16, pix)) - iota((16, pix), 0) // planes
-    ).astype(F32).astype(BF16)
-    nothing = jnp.zeros((16, pix), BF16)
-    rows = n_tr * planes
+    which16 = jnp.broadcast_to(which, (16, pix))
+    mine16 = (which16 - sub16 // planes).astype(F32).astype(BF16)
+    rows = n_tr // 2 * planes
 
     def spread_by_owner(values, at):
         twice = jnp.concatenate([values] * pair, axis=0)
-        for o in range(0, n_tr, pair):
+        for o in range(0, n_tr // 2, pair):
             xp[at + o * planes:at + (o + pair) * planes, :] = jnp.where(
-                owner16 == jnp.asarray(o, BF16), twice, nothing
+                mine16 == jnp.asarray(o, BF16), twice, nothing
             )
+
+    def pack(count):
+        packed = lax.dot_general(
+            xp[0:2 * count, :], hot_slot[...], NT, preferred_element_type=F32
+        )
+        return packed[0:count] + packed[count:2 * count]
+
+    def of_owner(packed, o, at, height):
+        return packed[at:at + height, (o % 2) * CAP:(o % 2 + 1) * CAP]
 
     for load in loads[1:]:
         load.wait()
     weight = weight_ref[...]
     wa, wb = two_pieces(weight)
     ca, cb = two_pieces(cell_ref[...].astype(F32))
-    extra = rows + n_tr
+    extra = rows + 16
     spread_by_owner(wa, 0)
     spread_by_owner(wb, extra)
-    xp[rows:extra, :] = (hot * ca.astype(F32)).astype(BF16)
-    xp[extra + rows:2 * extra, :] = (hot * cb.astype(F32)).astype(BF16)
-    packed = lax.dot_general(xp[...], slot_hot, NT, preferred_element_type=F32)
-    packed = packed[0:extra] + packed[extra:2 * extra]
+    here16 = (which16 - sub16).astype(F32).astype(BF16) == jnp.asarray(0, BF16)
+    xp[rows:extra, :] = jnp.where(here16, jnp.broadcast_to(ca, (16, pix)), nothing)
+    xp[extra + rows:2 * extra, :] = jnp.where(here16, jnp.broadcast_to(cb, (16, pix)), nothing)
+    packed = pack(extra)
     for o in range(n_tr):
-        pw[o, 0:planes, :] = packed[o * planes:(o + 1) * planes]
-        pw[o, planes:planes + 1, :] = packed[rows + o:rows + o + 1]
+        pw[o, 0:planes, :] = of_owner(packed, o, o // 2 * planes, planes)
+        pw[o, planes:planes + 1, :] = of_owner(packed, o, rows + o // 2, 1)
 
     pl.semaphore_wait(barrier, n_tr - 1 + n_los - 1)
 
     routed = [None], [None]
+
+    orders = (
+        [*range(1, n_tr // 2), *range(n_tr - 1, n_tr // 2 - 1, -1)],
+        [*range(1, n_tr // 4), *range(n_tr - 1, n_tr // 4 - 1, -1)],
+    )
 
     def route(stage, packs, into):
         for slot in range(1, n_tr):
@@ -164,8 +188,8 @@
                 packs.at[peer], into.at[slot],
                 route_send.at[stage, slot], route_recv.at[stage, slot], peer, los,
             ))
-        for copy in routed[stage][:0:-1]:
-            copy.start()
+        for slot in orders[stage]:
+            routed[stage][slot].start()
 
     route(0, pw, rw)
     rw[0] = pw[tr]
@@ -173,10 +197,9 @@
     fa, fb = two_pieces(flux_ref[...] * weight)
     spread_by_owner(fa, 0)
     spread_by_owner(fb, rows)
-    packed = lax.dot_general(xp[0:2 * rows, :], slot_hot, NT, preferred_element_type=F32)
-    packed = packed[0:rows] + packed[rows:2 * rows]
+    packed = pack(rows)
     for o in range(n_tr):
-        pf[o] = packed[o * planes:(o + 1) * planes]
+        pf[o] = of_owner(packed, o, o // 2 * planes, planes)
     route(1, pf, rf)
     rf[0] = pf[tr]
 
@@ -201,24 +224,27 @@
     each = SX * planes
     full = n_los * each
     upper = iota((8, span), 0) < SX
-    low_iota = iota((CHUNK, span), 0)
-    row16 = iota((16, span), 0) % SX
+    sub_span = iota((16, span), 0)
+    row16 = sub_span % SX
+    ones = jnp.ones((16, span), BF16)
     none = jnp.zeros((16, span), BF16)
     upper3 = iota((planes // 2, 8, 128), 1) < SX
 
-    def scatter(stage, arrived):
-        for g in range(chunks - 1, -1, -1):
+    def scatter(stage, g):
+        arrived = (rw, rf)[stage]
+
+        def build():
             slots = range(g * jump, (g + 1) * jump)
-            for slot in reversed(slots):
-                if slot:
-                    routed[stage][slot].wait_recv()
             if stage == 0:
                 cell = jnp.concatenate([arrived[t, planes:planes + 1, :] for t in slots], axis=1)
                 cell = (cell + 0.5).astype(I32)
                 col = cell % width
                 place = (col // CHUNK) * SX + cell // width
-                low = jnp.broadcast_to(col % CHUNK, (CHUNK, span))
-                lows[g] = jnp.where(low_iota == low, 1.0, 0.0).astype(BF16)
+                low = (
+                    jnp.broadcast_to(col % CHUNK, (16, span)) - sub_span
+                ).astype(F32).astype(BF16)
+                for t in range(0, CHUNK, 16):
+                    lows[g, t:t + 16, :] = jnp.where(low == jnp.asarray(t, BF16), ones, none)
                 dests[g] = (
                     jnp.broadcast_to(place, (16, span)) - row16
                 ).astype(F32).astype(BF16)
@@ -236,20 +262,28 @@
                 mine = dest == jnp.asarray(SX * k, BF16)
                 for t in range(0, each, 16):
                     at = k * each + t
-                    xs[at:at + 16, :] = jnp.where(mine, ba[t:t + 16], none)
-                    xs[full + at:full + at + 16, :] = jnp.where(mine, bb[t:t + 16], none)
-            part = lax.dot_general(xs[...], lows[g], NT, preferred_element_type=F32)
+                    xs[stage, at:at + 16, :] = jnp.where(mine, ba[t:t + 16], none)
+                    xs[stage, full + at:full + at + 16, :] = jnp.where(mine, bb[t:t + 16], none)
+
+        def add():
+            part = lax.dot_general(xs[stage], lows[g], NT, preferred_element_type=F32)
             part = part[0:full] + part[full:2 * full]
-            if g == chunks - 1:
-                acc[...] = part
+            if g == 0:
+                acc[stage] = part
             else:
-                acc[...] = acc[...] + part
+                acc[stage] = acc[stage] + part
+
+        for slot in range(g * jump, (g + 1) * jump):
+            if slot:
+                routed[stage][slot].wait_recv()
+        build()
+        add()
 
     here = pl.ds(los * planes, planes)
 
     def enter(stage, out, into):
         for k in range(n_los):
-            both = acc[k * each:(k + 1) * each, :]
+            both = acc[stage, k * each:(k + 1) * each, :]
             left = both[:, 0:128].reshape(planes // 2, 8, 128)
             right = both[:, 128:256].reshape(planes // 2, 8, 128)
             even = jnp.where(upper3, left, roll(right, 4, 1))
@@ -269,9 +303,15 @@
         into[here] = out[here]
         return copies
 
-    scatter(0, rw)
+    near = max(1, chunks // 2)
+    for g in range(near):
+        scatter(0, g)
+    scatter(1, 0)
+    for g in range(chunks - 1, near - 1, -1):
+        scatter(0, g)
     entered_w = enter(0, sw, tw)
-    scatter(1, rf)
+    for g in range(1, chunks):
+        scatter(1, g)
     entered_f = enter(1, sf, tf)
 
     for copy in entered_w:
@@ -368,18 +408,18 @@
             else:
                 pl.when(here_is != first)(copy.wait_recv)
 
-    wide = 8
+    wide = min(32, depth)
 
     def edge_rows(field, turn):
         def pack(block, none):
-            for i in range(2):
+            for i in range(wide // 4):
                 down = up = zero
                 for j in range(4):
                     v = field[block * wide + i * 4 + j]
                     down = jnp.where(quarter == j, roll(v, j - 3, 0), down)
                     up = jnp.where(quarter == j, roll(v, j, 0), up)
-                hs[turn, 0, block * 2 + i] = down
-                hs[turn, 1, block * 2 + i] = up
+                hs[turn, 0, block * (wide // 4) + i] = down
+                hs[turn, 1, block * (wide // 4) + i] = up
             return none
 
         lax.fori_loop(0, depth // wide, pack, 0)
@@ -421,7 +461,8 @@
             for i in range(wide):
                 zi = block * wide + i
                 j = i % 4
-                above, below = hr[turn, 0, block * 2 + i // 4], hr[turn, 1, block * 2 + i // 4]
+                four = block * (wide // 4) + i // 4
+                above, below = hr[turn, 0, four], hr[turn, 1, four]
                 rows = jnp.where(
                     first_row, roll(above, -j, 0), jnp.where(last_row, roll(below, 3 - j, 0), 0.0)
                 )
@@ -451,17 +492,17 @@
     dot_bz = solve(tf, zf)
     edge_rows(zf, 0)
     edge_columns(zf, 0)
+    operate_inside(zf, tf)
     left_z = leave(zf, 0)
-    operate_inside(zf, tf)
     edge_each(0, 0, "arrived")
     edge_each(0, 1, "arrived")
     dot_zq = operate_edges(zf, 0, qf)
     dot_qw = solve(qf, wf)
     edge_rows(wf, 1)
     edge_columns(wf, 1)
+    operate_inside(wf, qf)
     left_q = leave(qf, 1)
     left_w = leave(wf, 2)
-    operate_inside(wf, qf)
     edge_each(1, 0, "arrived")
     edge_each(1, 1, "arrived")
     dot_ws = operate_edges(wf, 1, vf)
@@ -553,15 +594,16 @@
             pltpu.VMEM((planes, pix), F32), pltpu.VMEM((planes, pix), F32),
             pltpu.VMEM((1, pix), I32), pltpu.VMEM((1, pix), I32),
             pltpu.SMEM(plane_bin.shape, I32), pltpu.SMEM(bin_coeffs.shape, F32),
-            pltpu.VMEM((2 * n_tr * (planes + 1), pix), BF16),
-            pltpu.VMEM((2 * n_los * each, span), BF16),
+            pltpu.VMEM((2 * (n_tr // 2 * planes + 16), pix), BF16),
+            pltpu.VMEM((2 * CAP, pix), BF16),
+            pltpu.VMEM((2, 2 * n_los * each, span), BF16),
             pltpu.VMEM((n_tr, planes + 1, CAP), F32),
             pltpu.VMEM((n_tr, planes, CAP), F32),
             pltpu.VMEM((n_tr, planes + 1, CAP), F32),
             pltpu.VMEM((n_tr, planes, CAP), F32),
             pltpu.VMEM((n_tr // jump, CHUNK, span), BF16),
             pltpu.VMEM((n_tr // jump, 16, span), BF16),
-            pltpu.VMEM((n_los * each, CHUNK), F32),
+            pltpu.VMEM((2, n_los * each, CHUNK), F32),
             field, field, field, field,
             field, field, field, field, field, field, field, field, field, field, field,
             pltpu.VMEM((2, 2, depth // 4, 8, 128), F32),

time: 52.6 us -> 51 us (0.970)
  Pallas kernels: 50.4 us -> 48.8 us
    pallas_call x1, Pallas kernels: 50.4 us -> 48.8 us  [local(): pl.pallas_call(functools.partial(kernel, n_tr, n_los, nzr), out_shape=(ou...]
where the time goes in v2:
time: 51 us; the launch traced here: 50.9 us
  Pallas kernels  48.8 us (96%)
  local copies, waits for them, and re-layouts  1.41 us (3%)
  between operations  0.64 us (1%)
    pallas_call x1, Pallas kernels, local(): pl.pallas_call(functools.partial(kernel, n_tr, n_los, nzr), out_shape=(ou...  48.8 us
    unnamed x2, local copies, waits for them, and re-layouts  1.41 us

profile of v2, /device:TPU:1, one launch (start us, length us, event | category | flops | bytes accessed | tf_op | source)
XLA Modules:
  0.0 50.9 jit_solution(10271113830503464444)
XLA Ops:
  0.6 48.8 %wiener.1 = (f32[8,4,2048]{2,1,0:T(4,128)S(1)}, f32[8,4,2048]{2,1,0:T(4,128)S(1)}) custom-call(f32[8,2048]{1,0:T(8,128)} %flux_hbm.1, f32[8,2048]{1,0:T(8,128)} %weight_hbm.1, s32[1,2048]{1,0:T(1,128)} %bitcast.2, s32[1,2048]{1,0:T(1,128)} %bitcast.3, s32[64]{0:T(128)} %bin_hbm.1, f32[3,8]{1,0:T(4,128)} %coef_hbm.1), custom_call_target="tpu_custom_call" | custom-call | tf_op jit(solution)/shard_map/wiener/pallas_call | solution.py:588
  49.5 0.7 %copy.10 = f32[8,4,2048]{2,1,0:T(4,128)} copy(f32[8,4,2048]{2,1,0:T(4,128)S(1)} %get-tuple-element.4) | data formatting | bytes 524288
  50.2 0.7 %copy.11 = f32[8,4,2048]{2,1,0:T(4,128)} copy(f32[8,4,2048]{2,1,0:T(4,128)S(1)} %get-tuple-element.5) | data formatting | bytes 524288

commit v3 on v2

--- a/solution.py
+++ b/solution.py
@@ -34,11 +34,11 @@
 
 def kernel(
     n_tr, n_los, nzr, flux_hbm, weight_hbm, owner_hbm, cell_hbm, bin_hbm, coef_hbm,
-    sol_ref, res_ref,
+    rb, sf, factors,
     flux_ref, weight_ref, owner_ref, cell_ref, bin_ref, coef_ref,
-    xp, hot_slot, xs, pw, pf, rw, rf, lows, dests, acc, sw, sf, tw, tf,
+    xp, hot_slot, xs, pw, pf, rw, rf, lows, dests, acc, sw, tw, tf,
     kxs, kys, lks, base, inv, gf, zf, qf, wf, vf, pre,
-    hs, hr, cs, cr, rb, ps, p1, p2,
+    hs, hr, cs, cr, ps, p1, p2,
     load_sem, route_send, route_recv, in_send, in_recv, halo_send, halo_recv,
     out_send, out_recv, sum_send, sum_recv, fin_send, fin_recv,
 ):
@@ -304,13 +304,10 @@
         return copies
 
     near = max(1, chunks // 2)
-    for g in range(near):
-        scatter(0, g)
-    scatter(1, 0)
-    for g in range(chunks - 1, near - 1, -1):
+    for g in (*range(near), *range(chunks - 1, near - 1, -1)):
         scatter(0, g)
     entered_w = enter(0, sw, tw)
-    for g in range(1, chunks):
+    for g in range(chunks):
         scatter(1, g)
     entered_f = enter(1, sf, tf)
 
@@ -507,8 +504,14 @@
     edge_each(1, 1, "arrived")
     dot_ws = operate_edges(wf, 1, vf)
 
+    mixed = jnp.zeros((1, 128), F32)
+    lane1 = iota((1, 128), 1) // 32
     for n, dot in enumerate((dot_bz, dot_zq, dot_qw, dot_ws)):
-        ps[0, n:n + 1, :] = jnp.sum(dot, axis=0, keepdims=True)
+        row = jnp.sum(dot, axis=0, keepdims=True)
+        row = row + roll(row, 64, 1)
+        row = row + roll(row, 32, 1)
+        mixed = jnp.where(lane1 == n, row, mixed)
+    ps[0] = mixed
     summed = []
     for slot in range(n_tr - 1, 0, -1):
         copy = send(
@@ -518,6 +521,12 @@
         summed.append(copy)
     left_v = leave(vf, 3)
     total = ps[0]
+    for copies in (routed[0][1:], routed[1][1:], entered_w, entered_f, left_z):
+        for copy in copies:
+            copy.wait_send()
+    for turn in range(2):
+        for kind in range(2):
+            edge_each(turn, kind, "sent")
     for copy in summed:
         copy.wait_recv()
     for slot in range(1, n_tr):
@@ -534,9 +543,11 @@
         copy.wait_recv()
     for step in range(1, n_los):
         total = total + p2[step]
-    total = jnp.sum(total, axis=1, keepdims=True)
     bz, zq, qw, ws = (
-        jnp.broadcast_to(total[n:n + 1], (8, 128)) for n in range(4)
+        jnp.broadcast_to(
+            jnp.sum(jnp.where(lane1 == n, total, 0.0), axis=1, keepdims=True), (8, 128)
+        )
+        for n in range(4)
     )
     alpha = bz / zq
     rz = alpha * alpha * qw - bz
@@ -550,25 +561,25 @@
         for copy in copies:
             copy.wait_recv()
 
-    def finish(k, none):
+    factors[0] = main
+    factors[1] = other
+
+    for copies in (left_q, left_w, left_v, summed, finals):
+        for copy in copies:
+            copy.wait_send()
+
+
+def finish(rb, bf, factors, sol_ref, res_ref):
+    main, other = factors[0], factors[1]
+    n_los, planes = rb.shape[1:3]
+    for k in range(n_los):
         for p in range(planes):
             x = main * rb[0, k, p] - other * rb[2, k, p]
-            r = sf[k * planes + p] - main * rb[1, k, p] + other * rb[3, k, p]
+            r = bf[k * planes + p] - main * rb[1, k, p] + other * rb[3, k, p]
             for part in range(2):
-                at = pl.ds(pl.multiple_of(k * CHUNK + part * 128, 128), 128)
+                at = slice(k * CHUNK + part * 128, k * CHUNK + part * 128 + 128)
                 sol_ref[p, :, at] = x[part * SX:(part + 1) * SX]
                 res_ref[p, :, at] = r[part * SX:(part + 1) * SX]
-        return none
-
-    lax.fori_loop(0, n_los, finish, 0)
-
-    for copies in (routed[0][1:], routed[1][1:], entered_w, entered_f,
-                   left_z, left_q, left_w, left_v, summed, finals):
-        for copy in copies:
-            copy.wait_send()
-    for turn in range(2):
-        for kind in range(2):
-            edge_each(turn, kind, "sent")
 
 
 def local(flux, noise_weight, pixel_owner, pixel_cell, plane_bin, bin_coeffs):
@@ -585,11 +596,15 @@
     vmem = pl.BlockSpec(memory_space=pltpu.VMEM)
     hbm = pl.BlockSpec(memory_space=pltpu.MemorySpace.HBM)
     out = jax.ShapeDtypeStruct((planes, SX, cols), F32)
-    return pl.pallas_call(
+    fields, right_side, factors = pl.pallas_call(
         functools.partial(kernel, n_tr, n_los, nzr),
-        out_shape=(out, out),
+        out_shape=(
+            jax.ShapeDtypeStruct((4, n_los, planes, 8, 128), F32),
+            jax.ShapeDtypeStruct((depth, 8, 128), F32),
+            jax.ShapeDtypeStruct((2, 8, 128), F32),
+        ),
         in_specs=[hbm] * 6,
-        out_specs=(vmem, vmem),
+        out_specs=(vmem, vmem, vmem),
         scratch_shapes=[
             pltpu.VMEM((planes, pix), F32), pltpu.VMEM((planes, pix), F32),
             pltpu.VMEM((1, pix), I32), pltpu.VMEM((1, pix), I32),
@@ -604,16 +619,15 @@
             pltpu.VMEM((n_tr // jump, CHUNK, span), BF16),
             pltpu.VMEM((n_tr // jump, 16, span), BF16),
             pltpu.VMEM((2, n_los * each, CHUNK), F32),
-            field, field, field, field,
+            field, field, field,
             field, field, field, field, field, field, field, field, field, field, field,
             pltpu.VMEM((2, 2, depth // 4, 8, 128), F32),
             pltpu.VMEM((2, 2, depth // 4, 8, 128), F32),
             pltpu.VMEM((2, 8, 128), F32),
             pltpu.VMEM((2, 2, 8, 128), F32),
-            pltpu.VMEM((4, n_los, planes, 8, 128), F32),
-            pltpu.VMEM((2, 4, 128), F32),
-            pltpu.VMEM((n_tr, 4, 128), F32),
-            pltpu.VMEM((n_los, 4, 128), F32),
+            pltpu.VMEM((2, 1, 128), F32),
+            pltpu.VMEM((n_tr, 1, 128), F32),
+            pltpu.VMEM((n_los, 1, 128), F32),
             dma((6,)), dma((2, n_tr)), dma((2, n_tr)), dma((2, n_los)), dma((2, n_los)),
             dma((2, 2, 2)), dma((2, 2, 2)), dma((4, n_los)), dma((4, n_los)),
             dma((n_tr,)), dma((n_tr,)), dma((n_los,)), dma((n_los,)),
@@ -629,6 +643,15 @@
         ))
     )
 
+    return pl.pallas_call(
+        finish,
+        out_shape=(out, out),
+        in_specs=[vmem] * 3,
+        out_specs=(vmem, vmem),
+        compiler_params=pltpu.CompilerParams(vmem_limit_bytes=4 * 1024 * 1024),
+        name="finish",
+    )(fields, right_side, factors)
+
 
 def solution(mesh):
     placed = (P("los", "tr"), P("los", "tr"), P("tr", None), P("tr"), P(), P())

time: 51 us -> 50.3 us (0.986)
  local copies, waits for them, and re-layouts: 1.41 us -> 0 us
  Pallas kernels: 48.8 us -> 49.6 us
    unnamed x2 -> x0, local copies, waits for them, and re-layouts: 1.41 us -> none
    pallas_call x1 -> x2, Pallas kernels: 48.8 us -> 49.6 us  [the longest x1 48.7 us: local(): pl.pallas_call(functools.partial(kernel, n_tr, n_los, nzr), out_shape=(ja...]
where the time goes in v3:
time: 50.3 us; the launch traced here: 50.2 us
  Pallas kernels  49.6 us (99%)
  between operations  0.64 us (1%)
    pallas_call x1, Pallas kernels, local(): pl.pallas_call(functools.partial(kernel, n_tr, n_los, nzr), out_shape=(ja...  48.7 us

profile of v3, /device:TPU:1, one launch (start us, length us, event | category | flops | bytes accessed | tf_op | source)
XLA Modules:
  0.0 50.2 jit_solution(2868113609513677178)
XLA Ops:
  0.6 48.7 %wiener.1 = (f32[4,8,8,8,128]{4,3,2,1,0:T(8,128)S(1)}, f32[64,8,128]{2,1,0:T(8,128)S(1)}, f32[2,8,128]{2,1,0:T(8,128)S(1)}) custom-call(f32[8,2048]{1,0:T(8,128)} %flux_hbm.1, f32[8,2048]{1,0:T(8,128)} %weight_hbm.1, s32[1,2048]{1,0:T(1,128)} %bitcast.2, s32[1,2048]{1,0:T(1,128)} %bitcast.3, s32[64]{0:T(128)} %bin_hbm.1, f32[3,8]{1,0:T(4,128)} %coef_hbm.1), custom_call_target="tpu_custom_call" | custom-call | tf_op jit(solution)/shard_map/wiener/pallas_call | solution.py:599
  49.3 0.9 %finish.1 = (f32[8,4,2048]{2,1,0:T(4,128)}, f32[8,4,2048]{2,1,0:T(4,128)}) custom-call(f32[4,8,8,8,128]{4,3,2,1,0:T(8,128)S(1)} %get-tuple-element.5.rb, f32[64,8,128]{2,1,0:T(8,128)S(1)} %get-tuple-element.6.bf, f32[2,8,128]{2,1,0:T(8,128)S(1)} %get-tuple-element.7.factors), custom_call_target="tpu_custom_call" | custom-call | tf_op jit(solution)/shard_map/finish/pallas_call | solution.py:646

commit v4 on v3

--- a/solution.py
+++ b/solution.py
@@ -22,6 +22,12 @@
     return lax.broadcasted_iota(I32, shape, dim)
 
 
+def tree(parts):
+    while len(parts) > 1:
+        parts = [sum(parts[i + 1:i + 2], parts[i]) for i in range(0, len(parts), 2)]
+    return parts[0]
+
+
 def two_pieces(values):
     high = values.astype(BF16)
     return high, (values - high.astype(F32)).astype(BF16)
@@ -36,7 +42,7 @@
     n_tr, n_los, nzr, flux_hbm, weight_hbm, owner_hbm, cell_hbm, bin_hbm, coef_hbm,
     rb, sf, factors,
     flux_ref, weight_ref, owner_ref, cell_ref, bin_ref, coef_ref,
-    xp, hot_slot, xs, pw, pf, rw, rf, lows, dests, acc, sw, tw, tf,
+    hot_slot, pw, pf, rw, rf, lows, dests, acc, sw, tw, tf,
     kxs, kys, lks, base, inv, gf, zf, qf, wf, vf, pre,
     hs, hr, cs, cr, ps, p1, p2,
     load_sem, route_send, route_recv, in_send, in_recv, halo_send, halo_recv,
@@ -140,17 +146,18 @@
     mine16 = (which16 - sub16 // planes).astype(F32).astype(BF16)
     rows = n_tr // 2 * planes
 
-    def spread_by_owner(values, at):
+    def spread_by_owner(values):
         twice = jnp.concatenate([values] * pair, axis=0)
-        for o in range(0, n_tr // 2, pair):
-            xp[at + o * planes:at + (o + pair) * planes, :] = jnp.where(
-                mine16 == jnp.asarray(o, BF16), twice, nothing
-            )
-
-    def pack(count):
+        return [
+            jnp.where(mine16 == jnp.asarray(o, BF16), twice, nothing)
+            for o in range(0, n_tr // 2, pair)
+        ]
+
+    def pack(blocks):
         packed = lax.dot_general(
-            xp[0:2 * count, :], hot_slot[...], NT, preferred_element_type=F32
+            jnp.concatenate(blocks, axis=0), hot_slot[...], NT, preferred_element_type=F32
         )
+        count = packed.shape[0] // 2
         return packed[0:count] + packed[count:2 * count]
 
     def of_owner(packed, o, at, height):
@@ -161,13 +168,11 @@
     weight = weight_ref[...]
     wa, wb = two_pieces(weight)
     ca, cb = two_pieces(cell_ref[...].astype(F32))
-    extra = rows + 16
-    spread_by_owner(wa, 0)
-    spread_by_owner(wb, extra)
     here16 = (which16 - sub16).astype(F32).astype(BF16) == jnp.asarray(0, BF16)
-    xp[rows:extra, :] = jnp.where(here16, jnp.broadcast_to(ca, (16, pix)), nothing)
-    xp[extra + rows:2 * extra, :] = jnp.where(here16, jnp.broadcast_to(cb, (16, pix)), nothing)
-    packed = pack(extra)
+    packed = pack([
+        *spread_by_owner(wa), jnp.where(here16, jnp.broadcast_to(ca, (16, pix)), nothing),
+        *spread_by_owner(wb), jnp.where(here16, jnp.broadcast_to(cb, (16, pix)), nothing),
+    ])
     for o in range(n_tr):
         pw[o, 0:planes, :] = of_owner(packed, o, o // 2 * planes, planes)
         pw[o, planes:planes + 1, :] = of_owner(packed, o, rows + o // 2, 1)
@@ -195,9 +200,7 @@
     rw[0] = pw[tr]
 
     fa, fb = two_pieces(flux_ref[...] * weight)
-    spread_by_owner(fa, 0)
-    spread_by_owner(fb, rows)
-    packed = pack(rows)
+    packed = pack([*spread_by_owner(fa), *spread_by_owner(fb)])
     for o in range(n_tr):
         pf[o] = of_owner(packed, o, o // 2 * planes, planes)
     route(1, pf, rf)
@@ -258,15 +261,13 @@
                 for p in range(0, planes, 2)
             ], axis=0))
             dest = dests[g]
-            for k in range(n_los):
-                mine = dest == jnp.asarray(SX * k, BF16)
-                for t in range(0, each, 16):
-                    at = k * each + t
-                    xs[stage, at:at + 16, :] = jnp.where(mine, ba[t:t + 16], none)
-                    xs[stage, full + at:full + at + 16, :] = jnp.where(mine, bb[t:t + 16], none)
-
-        def add():
-            part = lax.dot_general(xs[stage], lows[g], NT, preferred_element_type=F32)
+            return jnp.concatenate([
+                jnp.where(dest == jnp.asarray(SX * k, BF16), piece[t:t + 16], none)
+                for piece in (ba, bb) for k in range(n_los) for t in range(0, each, 16)
+            ], axis=0)
+
+        def add(expanded):
+            part = lax.dot_general(expanded, lows[g], NT, preferred_element_type=F32)
             part = part[0:full] + part[full:2 * full]
             if g == 0:
                 acc[stage] = part
@@ -276,8 +277,7 @@
         for slot in range(g * jump, (g + 1) * jump):
             if slot:
                 routed[stage][slot].wait_recv()
-        build()
-        add()
+        add(build())
 
     here = pl.ds(los * planes, planes)
 
@@ -382,10 +382,14 @@
     inner_left, inner_right = (lane == 0) & ~in_half, (lane == 127) & in_half
     outer = ((lane == 0) & in_half) | ((lane == 127) & ~in_half)
 
+    wide = min(32, depth)
+    parts = depth // wide
+
     def edge_copy(turn, side, kind):
         step = 1 if side == 0 else -1
-        if kind == 0:
-            src, dst, where = hs.at[turn, side], hr.at[turn, side], (
+        if kind < parts:
+            piece = pl.ds(kind * (wide // 4), wide // 4)
+            src, dst, where = hs.at[turn, side, piece], hr.at[turn, side, piece], (
                 (tr + step + n_tr) % n_tr, los)
         else:
             src, dst, where = cs.at[turn], cr.at[turn, side], (tr, (los + step + n_los) % n_los)
@@ -396,7 +400,7 @@
     def edge_each(turn, kind, what):
         for side in range(2):
             copy = edge_copy(turn, side, kind)
-            here_is, size = (tr, n_tr) if kind == 0 else (los, n_los)
+            here_is, size = (tr, n_tr) if kind < parts else (los, n_los)
             first, last = (0, size - 1) if side == 0 else (size - 1, 0)
             if what == "start":
                 pl.when(here_is != last)(copy.start)
@@ -405,10 +409,9 @@
             else:
                 pl.when(here_is != first)(copy.wait_recv)
 
-    wide = min(32, depth)
 
     def edge_rows(field, turn):
-        def pack(block, none):
+        for block in range(parts):
             for i in range(wide // 4):
                 down = up = zero
                 for j in range(4):
@@ -417,10 +420,7 @@
                     up = jnp.where(quarter == j, roll(v, j, 0), up)
                 hs[turn, 0, block * (wide // 4) + i] = down
                 hs[turn, 1, block * (wide // 4) + i] = up
-            return none
-
-        lax.fori_loop(0, depth // wide, pack, 0)
-        edge_each(turn, 0, "start")
+            edge_each(turn, block, "start")
 
     def edge_columns(field, turn):
         def pack(block, found):
@@ -432,7 +432,7 @@
             return found
 
         cs[turn] = lax.fori_loop(0, depth // wide, pack, zero)
-        edge_each(turn, 1, "start")
+        edge_each(turn, parts, "start")
 
     def operate_inside(field, source):
         def some(block, none):
@@ -452,9 +452,11 @@
         lax.fori_loop(0, depth // wide, some, 0)
 
     def operate_edges(field, turn, out):
+        edge_each(turn, parts, "arrived")
         columns = jnp.where(in_half, cr[turn, 0], roll(cr[turn, 1], 127, 1))
-
-        def some(block, total):
+        total = zero
+        for block in range(parts):
+            edge_each(turn, block, "arrived")
             for i in range(wide):
                 zi = block * wide + i
                 j = i % 4
@@ -467,9 +469,7 @@
                 image = pre[zi] - (kxs[zi] * rows + kys[zi] * beside)
                 out[zi] = image
                 total = total + field[zi] * image
-            return total
-
-        return lax.fori_loop(0, depth // wide, some, zero)
+        return total
 
     def leave(field, which):
         copies = []
@@ -491,8 +491,6 @@
     edge_columns(zf, 0)
     operate_inside(zf, tf)
     left_z = leave(zf, 0)
-    edge_each(0, 0, "arrived")
-    edge_each(0, 1, "arrived")
     dot_zq = operate_edges(zf, 0, qf)
     dot_qw = solve(qf, wf)
     edge_rows(wf, 1)
@@ -500,18 +498,18 @@
     operate_inside(wf, qf)
     left_q = leave(qf, 1)
     left_w = leave(wf, 2)
-    edge_each(1, 0, "arrived")
-    edge_each(1, 1, "arrived")
-    dot_ws = operate_edges(wf, 1, vf)
-
-    mixed = jnp.zeros((1, 128), F32)
     lane1 = iota((1, 128), 1) // 32
-    for n, dot in enumerate((dot_bz, dot_zq, dot_qw, dot_ws)):
+
+    def part_of(dot):
         row = jnp.sum(dot, axis=0, keepdims=True)
         row = row + roll(row, 64, 1)
-        row = row + roll(row, 32, 1)
-        mixed = jnp.where(lane1 == n, row, mixed)
-    ps[0] = mixed
+        return row + roll(row, 32, 1)
+
+    mixed = jnp.where(lane1 == 0, part_of(dot_bz), part_of(dot_zq))
+    mixed = jnp.where(lane1 == 2, part_of(dot_qw), mixed)
+    dot_ws = operate_edges(wf, 1, vf)
+
+    ps[0] = jnp.where(lane1 == 3, part_of(dot_ws), mixed)
     summed = []
     for slot in range(n_tr - 1, 0, -1):
         copy = send(
@@ -525,12 +523,11 @@
         for copy in copies:
             copy.wait_send()
     for turn in range(2):
-        for kind in range(2):
+        for kind in range(parts + 1):
             edge_each(turn, kind, "sent")
     for copy in summed:
         copy.wait_recv()
-    for slot in range(1, n_tr):
-        total = total + p1[slot]
+    total = tree([total, *(p1[slot] for slot in range(1, n_tr))])
     ps[1] = total
     finals = []
     for step in far_steps:
@@ -541,8 +538,7 @@
         finals.append(copy)
     for copy in finals:
         copy.wait_recv()
-    for step in range(1, n_los):
-        total = total + p2[step]
+    total = tree([total, *(p2[step] for step in range(1, n_los))])
     bz, zq, qw, ws = (
         jnp.broadcast_to(
             jnp.sum(jnp.where(lane1 == n, total, 0.0), axis=1, keepdims=True), (8, 128)
@@ -609,9 +605,7 @@
             pltpu.VMEM((planes, pix), F32), pltpu.VMEM((planes, pix), F32),
             pltpu.VMEM((1, pix), I32), pltpu.VMEM((1, pix), I32),
             pltpu.SMEM(plane_bin.shape, I32), pltpu.SMEM(bin_coeffs.shape, F32),
-            pltpu.VMEM((2 * (n_tr // 2 * planes + 16), pix), BF16),
             pltpu.VMEM((2 * CAP, pix), BF16),
-            pltpu.VMEM((2, 2 * n_los * each, span), BF16),
             pltpu.VMEM((n_tr, planes + 1, CAP), F32),
             pltpu.VMEM((n_tr, planes, CAP), F32),
             pltpu.VMEM((n_tr, planes + 1, CAP), F32),
@@ -629,7 +623,7 @@
             pltpu.VMEM((n_tr, 1, 128), F32),
             pltpu.VMEM((n_los, 1, 128), F32),
             dma((6,)), dma((2, n_tr)), dma((2, n_tr)), dma((2, n_los)), dma((2, n_los)),
-            dma((2, 2, 2)), dma((2, 2, 2)), dma((4, n_los)), dma((4, n_los)),
+            dma((2, 2, 3)), dma((2, 2, 3)), dma((4, n_los)), dma((4, n_los)),
             dma((n_tr,)), dma((n_tr,)), dma((n_los,)), dma((n_los,)),
         ],
         compiler_params=pltpu.CompilerParams(

time: 50.3 us -> 50 us (level)
  no operation moved by 1% of the time
where the time goes in v4:
time: 50 us; the launch traced here: 49.9 us
  Pallas kernels  49.2 us (98%)
  between operations  0.64 us (1%)
    pallas_call x1, Pallas kernels, local(): pl.pallas_call(functools.partial(kernel, n_tr, n_los, nzr), out_shape=(ja...  48.3 us

profile of v4, /device:TPU:1, one launch (start us, length us, event | category | flops | bytes accessed | tf_op | source)
XLA Modules:
  0.0 49.9 jit_solution(15197383812196208145)
XLA Ops:
  0.6 48.3 %wiener.1 = (f32[4,8,8,8,128]{4,3,2,1,0:T(8,128)S(1)}, f32[64,8,128]{2,1,0:T(8,128)S(1)}, f32[2,8,128]{2,1,0:T(8,128)S(1)}) custom-call(f32[8,2048]{1,0:T(8,128)} %flux_hbm.1, f32[8,2048]{1,0:T(8,128)} %weight_hbm.1, s32[1,2048]{1,0:T(1,128)} %bitcast.2, s32[1,2048]{1,0:T(1,128)} %bitcast.3, s32[64]{0:T(128)} %bin_hbm.1, f32[3,8]{1,0:T(4,128)} %coef_hbm.1), custom_call_target="tpu_custom_call" | custom-call | tf_op jit(solution)/shard_map/wiener/pallas_call | solution.py:595
  49.0 0.9 %finish.1 = (f32[8,4,2048]{2,1,0:T(4,128)}, f32[8,4,2048]{2,1,0:T(4,128)}) custom-call(f32[4,8,8,8,128]{4,3,2,1,0:T(8,128)S(1)} %get-tuple-element.5.rb, f32[64,8,128]{2,1,0:T(8,128)S(1)} %get-tuple-element.6.bf, f32[2,8,128]{2,1,0:T(8,128)S(1)} %get-tuple-element.7.factors), custom_call_target="tpu_custom_call" | custom-call | tf_op jit(solution)/shard_map/finish/pallas_call | solution.py:640
